TPU v7x, 32 devices: a whole 2x2x4 slice. The times are simulated.
32 devices in a mesh: feat: 2 (over y), node: 16 (over z, x, core).
Axes of the slice: x: 2, y: 2, z: 4, core: 2. Of those that a mesh axis runs over, the one named last changes fastest.
Arguments:
- features: bfloat16 [32768, 4096], P('node', 'feat'), may hold values from -6 to 6
- seed_feats: bfloat16 [2048, 4096], P('node', 'feat'), may hold values from -6 to 6
- patterns: int32 [256, 8, 128, 8], P('node'), may hold values from 0 to 65535, as said below
- sources: int32 [256, 8], P('node'), may hold values from 0 to 15
- counts: int32 [256], P('node'), may hold values from 1 to 8
- w_self: bfloat16 [4096, 1024], P('feat'), may hold values from -0.09375 to 0.09375
- w_neigh: bfloat16 [4096, 1024], P('feat'), may hold values from -0.09375 to 0.09375
- bias_term: float32 [1024], replicated, may hold values from -3 to 3
- out_grad: bfloat16 [2048, 1024], P('node'), may hold values from -0.5 to 0.5
Outputs:
- hidden: bfloat16 [2048, 1024], P('node')
- grad_self: float32 [4096, 1024], P(('feat', 'node'))
- grad_neigh: float32 [4096, 1024], P(('feat', 'node'))
- grad_bias: float32 [1024], P('node')
Inputs may be any that keep to these rules, and one draw needn't show every extreme that they name: `patterns`: each word holds 16 entries of 0 or 1 in its 16 low bits.
All inputs are finite; a program needn't handle non-finite values.
Results may differ from a plain program's by a relative error of at most 0.024.
The roundings to bfloat16 on the way count: a program that leaves them out, or rounds other values in their place, can miss the bound.
Values may be sent and summed in bfloat16 or wider, within the bound.
A program may use at most 128 MiB of HBM per device.

v0:
```python
import jax
import jax.numpy as jnp
from jax import lax
from jax.sharding import PartitionSpec as P


def unpack(packed):
    shifts = jnp.arange(16, dtype=jnp.int32)
    bit_values = jnp.bitwise_and(jnp.right_shift(packed[..., None], shifts), 1)
    return bit_values.reshape(packed.shape[:-1] + (packed.shape[-1] * 16,)).astype(jnp.bfloat16)


def body(features, seed_feats, patterns, sources, counts, w_self, w_neigh, bias_term, out_grad):
    targets = patterns.shape[0]
    fan_slots = patterns.shape[1]
    block_rows = patterns.shape[2]
    local_blocks = features.shape[0] // block_rows
    live_mask = jnp.arange(fan_slots, dtype=jnp.int32)[None, :] < counts[:, None]
    tile_bits = unpack(patterns) * live_mask[:, :, None, None].astype(jnp.bfloat16)
    source_pick = (
        sources[:, :, None] == jnp.arange(local_blocks, dtype=jnp.int32)[None, None, :]
    ).astype(jnp.bfloat16)
    mixing = jnp.einsum(
        "tkrs,tkb->trbs", tile_bits, source_pick, preferred_element_type=jnp.bfloat16
    )
    mixing = mixing.reshape(targets * block_rows, local_blocks * block_rows)
    summed_rows = jnp.dot(mixing, features, preferred_element_type=jnp.float32)
    degree = jnp.sum(mixing, axis=1, dtype=jnp.float32)
    owner_sums, owner_counts = (
        lax.psum_scatter(summed_rows, "node", scatter_dimension=0, tiled=True),
        lax.psum_scatter(degree, "node", scatter_dimension=0, tiled=True),
    )
    aggregate = (owner_sums / jnp.sqrt(1.0 + owner_counts)[:, None]).astype(jnp.bfloat16)
    local_pre = jnp.dot(seed_feats, w_self, preferred_element_type=jnp.float32)
    local_pre = local_pre + jnp.dot(aggregate, w_neigh, preferred_element_type=jnp.float32)
    pre_act = lax.psum(local_pre, "feat")
    hidden = jnp.maximum(pre_act + bias_term, 0.0).astype(jnp.bfloat16)
    grad_rows = jnp.where(hidden > 0, out_grad, jnp.zeros_like(out_grad))
    contract_rows = (((0,), (0,)), ((), ()))
    grad_self = lax.dot_general(
        seed_feats, grad_rows, contract_rows, preferred_element_type=jnp.float32
    )
    grad_neigh = lax.dot_general(
        aggregate, grad_rows, contract_rows, preferred_element_type=jnp.float32
    )
    grad_bias = jnp.sum(grad_rows.astype(jnp.float32), axis=0)
    grad_self, grad_neigh, grad_bias = (
        lax.psum_scatter(grad_self, "node", scatter_dimension=0, tiled=True),
        lax.psum_scatter(grad_neigh, "node", scatter_dimension=0, tiled=True),
        lax.psum_scatter(grad_bias, "node", scatter_dimension=0, tiled=True),
    )
    return (hidden, grad_self, grad_neigh, grad_bias)


def solution(mesh):
    return jax.shard_map(
        body,
        mesh=mesh,
        in_specs=(
            P("node", "feat"),
            P("node", "feat"),
            P("node", None, None, None),
            P("node", None),
            P("node"),
            P("feat", None),
            P("feat", None),
            P(),
            P("node", None),
        ),
        out_specs=(
            P("node", None),
            P(("feat", "node"), None),
            P(("feat", "node"), None),
            P("node"),
        ),
        check_vma=False,
    )
```

profile of v0, /device:TPU:0, one launch (start us, length us, event | category | flops | bytes accessed | tf_op | source)
XLA Modules:
  0.0 496.2 jit_solution(2182428408044448951)
XLA Ops:
  7.2 0.0 copy-start
  7.2 0.0 copy-start.5
  7.2 0.0 reduce-scatter.4.cloned.1.call-start
  7.2 0.1 shift_right_arithmetic.23
  7.3 0.7 fusion.10
  8.1 5.9 %fusion.5 = bf16[16,8,128,128]{2,3,1,0:T(8,128)(2,1)} fusion(s32[128]{0:T(128)S(1)} %shift_right_arithmetic.23, s32[16,8,128,8]{2,3,1,0:T(8,128)} %param.11, bf16[16,8]{1,0:T(8,128)(2,1)S(1)} %fusion.10), kind=kLoop, calls=%fused_computation.8 | loop fusion | flops 14680064 | bytes 4719360 | tf_op jit(solution)/shard_map/mul | solution.py:19
  13.9 6.7 %copy.20 = bf16[16,8,128,128]{3,1,2,0:T(8,128)(2,1)} copy(bf16[16,8,128,128]{2,3,1,0:T(8,128)(2,1)} %fusion.5) | data formatting | bytes 8388608 | tf_op jit(solution)/shard_map/mul | solution.py:19
  20.7 0.0 copy-done.5
  20.7 0.1 copy.19
  20.8 17.8 %convert_reduce_fusion = (f32[16,128]{1,0:T(8,128)S(1)}, bf16[16,16,128,128]{3,1,2,0:T(8,128)(2,1)S(1)}) fusion(bf16[16,8,128,128]{3,1,2,0:T(8,128)(2,1)} %copy.20, s32[16,8]{1,0:T(8,128)S(1)} %copy.19), kind=kOutput, calls=%fused_computation | convolution fusion | flops 75497472 | bytes 12591616 | tf_op jit(solution)/shard_map/tkrs,tkb->trbs/dot_general | solution.py:23
  38.6 21.7 %fusion = f32[2048,2048]{1,0:T(8,128)} fusion(bf16[2048,2048]{1,0:T(8,128)(2,1)} %param.9, bf16[256,8,16,128]{3,2,1,0:T(8,128)(2,1)S(1)} %bitcast.32), kind=kOutput, calls=%fused_computation.1 | convolution fusion | flops 17179869184 | bytes 33554432 | tf_op jit(solution)/shard_map/dot_general | solution.py:27
  60.3 0.0 copy-start.6
  60.3 0.0 reduce-scatter.4.cloned.1.call-update
  60.3 0.0 copy-start.1
  60.3 0.0 copy-start.4
  60.4 0.0 all-reduce.4.cloned.1.call-start
  60.4 0.6 copy-done.6
  61.0 0.6 dynamic-slice
  62.2 35.6 %all-reduce = f32[2048]{0:T(1024)S(1)} all-reduce(f32[2048]{0:T(1024)S(1)} %bitcast.33), channel_id=3, replica_groups=mesh['feat'=2,'node'=16] {'node'}, use_global_device_ids=true, to_apply=%region_2.0.clone | all-reduce | flops 2048 | bytes 16384
  97.8 0.1 fusion.11
  97.9 0.0 copy-done
  97.9 2.9 fusion.13
  100.8 139.7 %reduce-scatter.4.cloned.1.call-done = f32[128,2048]{1,0:T(8,128)} async-done(((f32[2048,2048]{1,0:T(8,128)}), f32[128,2048]{1,0:T(8,128)}) %reduce-scatter.4.cloned.1.call-update) | async-done | bytes 1048592 | tf_op jit(solution)/shard_map/reduce_scatter | solution.py:30
  240.6 4.1 convolution_add_fusion
  244.6 0.0 all-reduce.4.cloned.1.call-update
  244.7 0.0 reduce-scatter.6.cloned.1.call-start
  244.7 27.9 %all-reduce.4.cloned.1.call-done = f32[128,1024]{1,0:T(8,128)} async-done(((f32[128,1024]{1,0:T(8,128)}), f32[128,1024]{1,0:T(8,128)}) %all-reduce.4.cloned.1.call-update) | async-done | bytes 524304 | tf_op jit(solution)/shard_map/psum | solution.py:36
  272.6 0.0 copy-done.1
  272.6 0.0 copy-done.4
  272.6 1.2 convert_reduce_fusion.1
  273.8 0.0 copy-start.2
  273.8 0.0 copy-start.3
  273.8 4.5 convolution_bitcast_fusion
  278.3 0.0 reduce-scatter.6.cloned.1.call-update
  278.3 0.0 reduce-scatter.8.cloned.1.call-start
  278.4 0.0 copy-done.2
  278.4 0.0 copy-done.3
  278.4 4.6 fusion.12
  283.0 0.0 reduce-scatter.8.cloned.1.call-update
  283.6 33.6 %all-reduce.1 = f32[1024]{0:T(1024)S(1)} all-reduce(f32[1024]{0:T(1024)S(1)} %get-tuple-element.16), channel_id=6, replica_groups=mesh['feat'=2,'node'=16] {'node'}, use_global_device_ids=true, to_apply=%region_7.8.clone | all-reduce | flops 1024 | bytes 8192
  317.2 0.6 dynamic-slice.3
  317.8 64.3 %reduce-scatter.6.cloned.1.call-done = f32[128,1024]{0,1:T(8,128)} async-done(((f32[2048,1024]{0,1:T(8,128)}), f32[128,1024]{0,1:T(8,128)}) %reduce-scatter.6.cloned.1.call-update) | async-done | bytes 524304 | tf_op jit(solution)/shard_map/reduce_scatter | solution.py:48
  382.1 2.0 copy.21
  384.1 105.6 %reduce-scatter.8.cloned.1.call-done = f32[128,1024]{1,0:T(8,128)} async-done(((f32[2048,1024]{1,0:T(8,128)}), f32[128,1024]{1,0:T(8,128)}) %reduce-scatter.8.cloned.1.call-update) | async-done | bytes 524304 | tf_op jit(solution)/shard_map/reduce_scatter | solution.py:49
  (1 shorter events, 0.0 us)
Async XLA Ops:
  7.2 90.7 %copy-start = (bf16[128,2048]{1,0:T(8,128)(2,1)S(1)}, bf16[128,2048]{1,0:T(8,128)(2,1)}, u32[]{:S(2)}) copy-start(bf16[128,2048]{1,0:T(8,128)(2,1)} %param.10) | copy-start | bytes 1572868
  7.2 13.5 %copy-start.5 = (s32[16,8]{0,1:T(8,128)S(1)}, s32[16,8]{0,1:T(8,128)}, u32[]{:S(2)}) copy-start(s32[16,8]{0,1:T(8,128)} %param.12) | copy-start | bytes 1540
  7.2 233.4 %reduce-scatter.4.cloned.1.call-start = ((), (), s32[]{:S(2)}) async-start(), calls=%async_computation.3 | async-start | bytes 17825792 | tf_op jit(solution)/shard_map/reduce_scatter | solution.py:30
  60.3 0.7 copy-start.6
  60.3 212.3 %copy-start.1 = (bf16[128,1024]{1,0:T(8,128)(2,1)S(1)}, bf16[128,1024]{1,0:T(8,128)(2,1)}, u32[]{:S(2)}) copy-start(bf16[128,1024]{1,0:T(8,128)(2,1)} %param.17) | copy-start | bytes 786436
  60.3 212.2 %copy-start.4 = (f32[1024]{0:T(1024)S(1)}, f32[1024]{0:T(1024)}, u32[]{:S(2)}) copy-start(f32[1024]{0:T(1024)} %param.16) | copy-start | bytes 12292
  60.4 212.2 %all-reduce.4.cloned.1.call-start = ((), (), s32[]{:S(2)}) async-start(), calls=%async_computation.4 | async-start | bytes 1048576 | tf_op jit(solution)/shard_map/psum | solution.py:36
  244.7 137.4 %reduce-scatter.6.cloned.1.call-start = ((), (), s32[]{:S(2)}) async-start(), calls=%async_computation.5 | async-start | bytes 8912896 | tf_op jit(solution)/shard_map/reduce_scatter | solution.py:48
  273.8 4.6 copy-start.2
  273.8 4.6 copy-start.3
  278.3 211.3 %reduce-scatter.8.cloned.1.call-start = ((), (), s32[]{:S(2)}) async-start(), calls=%async_computation.6 | async-start | bytes 8912896 | tf_op jit(solution)/shard_map/reduce_scatter | solution.py:49
Sparse Core Ops, SparseCore 0:
  60.5 180.0 reduce-scatter.3
  244.8 27.7 all-reduce.3
  278.4 103.5 reduce-scatter.5
  386.6 103.0 reduce-scatter.7
where the time goes:
time: 497 us; the launch traced here: 496 us
  waiting for transfers between devices  337 us (68%)
  blocking collectives  69.2 us (14%)
  matrix products  55.6 us (11%)
  between operations  15.2 us (3%)
  local copies, waits for them, and re-layouts  10.7 us (2%)
  other arithmetic  7.86 us (2%)
    reduce_scatter x1, waiting for transfers between devices, body(): lax.psum_scatter(summed_rows, 'node', scatter_dimension=0, tiled=True)  140 us
    reduce_scatter x1, waiting for transfers between devices, body(): lax.psum_scatter(grad_neigh, 'node', scatter_dimension=0, tiled=True)  106 us
    unnamed x2, blocking collectives  69.2 us
    reduce_scatter x1, waiting for transfers between devices, body(): lax.psum_scatter(grad_self, 'node', scatter_dimension=0, tiled=True)  64.3 us
    psum x1, waiting for transfers between devices, body(): pre_act = lax.psum(local_pre, 'feat')  27.9 us
    dot_general x1, matrix products, body(): summed_rows = jnp.dot(mixing, features, preferred_element_type=jnp.float32)  21.7 us
    dot_general x1, matrix products, body(): jnp.einsum('tkrs,tkb->trbs', tile_bits, source_pick, preferred_element_ty...  17.8 us
  transfers between devices with their start and end apart: 4, of which 4 were waited for; matrix products, arithmetic and copies ran while one was open for 2% of the time, Pallas kernels for 0%

commit v1 on v0

--- a/solution.py
+++ b/solution.py
@@ -15,6 +15,8 @@
     fan_slots = patterns.shape[1]
     block_rows = patterns.shape[2]
     local_blocks = features.shape[0] // block_rows
+    n_node = lax.axis_size("node")
+    node_idx = lax.axis_index("node")
     live_mask = jnp.arange(fan_slots, dtype=jnp.int32)[None, :] < counts[:, None]
     tile_bits = unpack(patterns) * live_mask[:, :, None, None].astype(jnp.bfloat16)
     source_pick = (
@@ -26,28 +28,30 @@
     mixing = mixing.reshape(targets * block_rows, local_blocks * block_rows)
     summed_rows = jnp.dot(mixing, features, preferred_element_type=jnp.float32)
     degree = jnp.sum(mixing, axis=1, dtype=jnp.float32)
-    owner_sums, owner_counts = (
-        lax.psum_scatter(summed_rows, "node", scatter_dimension=0, tiled=True),
-        lax.psum_scatter(degree, "node", scatter_dimension=0, tiled=True),
-    )
+    owner_sums = lax.psum_scatter(summed_rows, "node", scatter_dimension=0, tiled=True)
+    owner_counts = lax.psum_scatter(degree, "node", scatter_dimension=0, tiled=True)
     aggregate = (owner_sums / jnp.sqrt(1.0 + owner_counts)[:, None]).astype(jnp.bfloat16)
     local_pre = jnp.dot(seed_feats, w_self, preferred_element_type=jnp.float32)
     local_pre = local_pre + jnp.dot(aggregate, w_neigh, preferred_element_type=jnp.float32)
     pre_act = lax.psum(local_pre, "feat")
     hidden = jnp.maximum(pre_act + bias_term, 0.0).astype(jnp.bfloat16)
     grad_rows = jnp.where(hidden > 0, out_grad, jnp.zeros_like(out_grad))
+    seed_cols = lax.all_to_all(seed_feats, "node", 1, 0, tiled=True)
+    agg_cols = lax.all_to_all(aggregate, "node", 1, 0, tiled=True)
+    grad_all = lax.all_gather(grad_rows, "node", axis=0, tiled=True)
     contract_rows = (((0,), (0,)), ((), ()))
     grad_self = lax.dot_general(
-        seed_feats, grad_rows, contract_rows, preferred_element_type=jnp.float32
+        seed_cols, grad_all, contract_rows, preferred_element_type=jnp.float32
     )
     grad_neigh = lax.dot_general(
-        aggregate, grad_rows, contract_rows, preferred_element_type=jnp.float32
+        agg_cols, grad_all, contract_rows, preferred_element_type=jnp.float32
     )
-    grad_bias = jnp.sum(grad_rows.astype(jnp.float32), axis=0)
-    grad_self, grad_neigh, grad_bias = (
-        lax.psum_scatter(grad_self, "node", scatter_dimension=0, tiled=True),
-        lax.psum_scatter(grad_neigh, "node", scatter_dimension=0, tiled=True),
-        lax.psum_scatter(grad_bias, "node", scatter_dimension=0, tiled=True),
+    hid_chunk = grad_all.shape[1] // n_node
+    grad_bias = jnp.sum(
+        lax.dynamic_slice_in_dim(grad_all, node_idx * hid_chunk, hid_chunk, axis=1).astype(
+            jnp.float32
+        ),
+        axis=0,
     )
     return (hidden, grad_self, grad_neigh, grad_bias)
 

time: 497 us -> 358 us (0.72)
  waiting for transfers between devices: 337 us -> 220 us
  blocking collectives: 69.2 us -> 35.6 us
  starting transfers between devices: 0.16 us -> 11.4 us
    reduce_scatter x2 -> x0, waiting for transfers between devices: 170 us -> none  [the longest x1 106 us: body(): lax.psum_scatter(grad_neigh, 'node', scatter_dimension=0, tiled=True)]
    unnamed x2 -> x1, blocking collectives: 69.2 us -> 35.6 us
    all_gather x0 -> x1, waiting for transfers between devices: none -> 32.4 us  [body(): grad_all = lax.all_gather(grad_rows, 'node', axis=0, tiled=True)]
    all_to_all x0 -> x2, waiting for transfers between devices: none -> 20.2 us  [the longest x1 20.2 us: body(): seed_cols = lax.all_to_all(seed_feats, 'node', 1, 0, tiled=True)]
    all_to_all x0 -> x2, starting transfers between devices: none -> 11.3 us  [the longest x1 5.64 us: body(): agg_cols = lax.all_to_all(aggregate, 'node', 1, 0, tiled=True)]
  transfers between devices with their start and end apart: 4 -> 5, of which waited for: 4 -> 4; matrix products, arithmetic and copies ran while one was open for 2% -> 3% of each run, Pallas kernels for 0% -> 0%
where the time goes in v1:
time: 358 us; the launch traced here: 357 us
  waiting for transfers between devices  220 us (61%)
  matrix products  53.8 us (15%)
  blocking collectives  35.6 us (10%)
  between operations  14.5 us (4%)
  other arithmetic  11.6 us (3%)
  starting transfers between devices  11.4 us (3%)
  local copies, waits for them, and re-layouts  10.4 us (3%)
    reduce_scatter x1, waiting for transfers between devices, body(): lax.psum_scatter(summed_rows, 'node', scatter_dimension=0, tiled=True)  140 us
    unnamed x1, blocking collectives  35.6 us
    all_gather x1, waiting for transfers between devices, body(): grad_all = lax.all_gather(grad_rows, 'node', axis=0, tiled=True)  32.4 us
    psum x1, waiting for transfers between devices, body(): pre_act = lax.psum(local_pre, 'feat')  27.9 us
    dot_general x1, matrix products, body(): summed_rows = jnp.dot(mixing, features, preferred_element_type=jnp.float32)  21.7 us
    all_to_all x1, waiting for transfers between devices, body(): seed_cols = lax.all_to_all(seed_feats, 'node', 1, 0, tiled=True)  20.2 us
    dot_general x1, matrix products, body(): jnp.einsum('tkrs,tkb->trbs', tile_bits, source_pick, preferred_element_ty...  17.8 us
  transfers between devices with their start and end apart: 5, of which 4 were waited for; matrix products, arithmetic and copies ran while one was open for 3% of the time, Pallas kernels for 0%

profile of v1, /device:TPU:0, one launch (start us, length us, event | category | flops | bytes accessed | tf_op | source)
XLA Modules:
  0.0 357.5 jit_solution(3109192281458399594)
XLA Ops:
  7.2 0.0 reduce-scatter.2.cloned.1.call-start
  7.2 0.1 shift_right_arithmetic.23
  7.3 0.7 fusion.10
  8.0 5.9 %fusion.5 = bf16[16,8,128,128]{2,3,1,0:T(8,128)(2,1)} fusion(s32[128]{0:T(128)S(1)} %shift_right_arithmetic.23, s32[16,8,128,8]{2,3,1,0:T(8,128)} %param.11, bf16[16,8]{1,0:T(8,128)(2,1)S(1)} %fusion.10), kind=kLoop, calls=%fused_computation.7 | loop fusion | flops 14680064 | bytes 4719360 | tf_op jit(solution)/shard_map/mul | solution.py:21
  13.9 0.0 copy-start.4
  13.9 6.8 %copy.27 = bf16[16,8,128,128]{3,1,2,0:T(8,128)(2,1)} copy(bf16[16,8,128,128]{2,3,1,0:T(8,128)(2,1)} %fusion.5) | data formatting | bytes 8388608 | tf_op jit(solution)/shard_map/mul | solution.py:21
  20.7 0.0 copy-done.4
  20.7 0.1 copy.26
  20.8 17.8 %convert_reduce_fusion = (f32[16,128]{1,0:T(8,128)S(1)}, bf16[16,16,128,128]{3,1,2,0:T(8,128)(2,1)S(1)}) fusion(bf16[16,8,128,128]{3,1,2,0:T(8,128)(2,1)} %copy.27, s32[16,8]{1,0:T(8,128)S(1)} %copy.26), kind=kOutput, calls=%fused_computation | convolution fusion | flops 75497472 | bytes 12591616 | tf_op jit(solution)/shard_map/tkrs,tkb->trbs/dot_general | solution.py:25
  38.6 21.7 %fusion = f32[2048,2048]{1,0:T(8,128)} fusion(bf16[2048,2048]{1,0:T(8,128)(2,1)} %param.9, bf16[256,8,16,128]{3,2,1,0:T(8,128)(2,1)S(1)} %bitcast.47), kind=kOutput, calls=%fused_computation.1 | convolution fusion | flops 17179869184 | bytes 33554432 | tf_op jit(solution)/shard_map/dot_general | solution.py:29
  60.3 0.0 copy-start.5
  60.4 0.0 copy-start
  60.4 0.0 reduce-scatter.2.cloned.1.call-update
  60.4 0.0 all-reduce.3.cloned.1.call-start
  60.4 0.6 copy-done.5
  61.0 0.6 dynamic-slice
  62.2 35.6 %all-reduce = f32[2048]{0:T(1024)S(1)} all-reduce(f32[2048]{0:T(1024)S(1)} %bitcast.51), channel_id=3, replica_groups=mesh['feat'=2,'node'=16] {'node'}, use_global_device_ids=true, to_apply=%region_2.0.clone | all-reduce | flops 2048 | bytes 16384
  97.9 0.1 fusion.11
  97.9 0.0 copy-done
  98.0 2.9 fusion.12
  100.9 0.0 copy-start.2
  100.9 0.0 copy-start.3
  100.9 139.7 %reduce-scatter.2.cloned.1.call-done = f32[128,2048]{1,0:T(8,128)} async-done(((f32[2048,2048]{1,0:T(8,128)}), f32[128,2048]{1,0:T(8,128)}) %reduce-scatter.2.cloned.1.call-update) | async-done | bytes 1048592 | tf_op jit(solution)/shard_map/reduce_scatter | solution.py:31
  240.6 0.0 copy-start.1
  240.6 4.2 %convolution_add_fusion = f32[128,1024]{1,0:T(8,128)} fusion(f32[128,1024]{1,0:T(8,128)S(1)} %fusion.12, bf16[2048,1024]{1,0:T(8,128)(2,1)} %param.15, f32[128,2048]{1,0:T(8,128)} %reduce-scatter.2.cloned.1.call-done, f32[128]{0:T(128)S(1)} %fusion.11), kind=kOutput, calls=%fused_computation.8 | convolution fusion | flops 537526272 | bytes 6291968 | tf_op jit(solution)/shard_map/dot_general | solution.py:35
  244.7 0.0 all-reduce.3.cloned.1.call-update
  244.8 0.0 all-gather.2.cloned.1.call-start
  244.8 27.9 %all-reduce.3.cloned.1.call-done = f32[128,1024]{1,0:T(8,128)} async-done(((f32[128,1024]{1,0:T(8,128)}), f32[128,1024]{1,0:T(8,128)}) %all-reduce.3.cloned.1.call-update) | async-done | bytes 524304 | tf_op jit(solution)/shard_map/psum | solution.py:36
  272.7 0.0 copy-done.2
  272.7 0.0 copy-done.3
  272.7 2.0 compare_select_fusion
  274.6 0.0 all-gather.2.cloned.1.call-update
  274.7 1.0 copy.28
  275.7 5.6 %all-to-all-start = ((bf16[128,16,128]{0,2,1:T(8,128)(2,1)}), bf16[128,16,128]{0,2,1:T(8,128)(2,1)S(1)}, u32[]{:S(2)}, u32[]{:S(2)}) async-start(bf16[128,16,128]{0,2,1:T(8,128)(2,1)} %bitcast.5), calls=%async_computation.1 | async-start | bytes 1048576 | tf_op jit(solution)/shard_map/all_to_all | solution.py:39
  281.3 0.0 copy-done.1
  281.3 1.0 copy_bitcast_fusion
  282.3 20.2 %all-to-all-done = bf16[128,16,128]{0,2,1:T(8,128)(2,1)S(1)} async-done(((bf16[128,16,128]{0,2,1:T(8,128)(2,1)}), bf16[128,16,128]{0,2,1:T(8,128)(2,1)S(1)}, u32[]{:S(2)}, u32[]{:S(2)}) %all-to-all-start) | async-done | bytes 524320 | tf_op jit(solution)/shard_map/all_to_all | solution.py:39
  302.5 5.6 %all-to-all-start.1 = ((bf16[128,16,128]{2,0,1:T(8,128)(2,1)}), bf16[128,16,128]{2,0,1:T(8,128)(2,1)S(1)}, u32[]{:S(2)}, u32[]{:S(2)}) async-start(bf16[128,16,128]{2,0,1:T(8,128)(2,1)} %copy_bitcast_fusion), calls=%async_computation.2 | async-start | bytes 1048576 | tf_op jit(solution)/shard_map/all_to_all | solution.py:40
  308.1 0.3 copy.29
  308.4 32.4 %all-gather.2.cloned.1.call-done = bf16[2048,1024]{1,0:T(8,128)(2,1)} async-done(((bf16[128,1024]{1,0:T(8,128)(2,1)}), bf16[2048,1024]{1,0:T(8,128)(2,1)}) %all-gather.2.cloned.1.call-update) | async-done | bytes 4194320 | tf_op jit(solution)/shard_map/all_gather | solution.py:41
  340.9 3.5 convolution_bitcast_fusion
  344.3 1.0 copy.31
  345.3 1.9 convert_reduce_fusion.1
  347.2 0.0 all-to-all-done.1
  347.2 3.7 %fusion.13 = f32[128,1024]{1,0:T(8,128)} fusion(bf16[2048,128]{1,0:T(8,128)(2,1)S(1)} %bitcast.48, bf16[2048,1024]{1,0:T(8,128)(2,1)} %all-gather.2.cloned.1.call-done), kind=kOutput, calls=%fused_computation.24 | convolution fusion | flops 536870912 | bytes 5242880 | tf_op jit(solution)/shard_map/dot_general | solution.py:46
  (1 shorter events, 0.0 us)
Async XLA Ops:
  7.2 233.4 %reduce-scatter.2.cloned.1.call-start = ((), (), s32[]{:S(2)}) async-start(), calls=%async_computation.3 | async-start | bytes 17825792 | tf_op jit(solution)/shard_map/reduce_scatter | solution.py:31
  13.9 6.8 %copy-start.4 = (s32[16,8]{0,1:T(8,128)S(1)}, s32[16,8]{0,1:T(8,128)}, u32[]{:S(2)}) copy-start(s32[16,8]{0,1:T(8,128)} %param.12) | copy-start | bytes 1540
  60.3 0.7 copy-start.5
  60.4 37.6 %copy-start = (bf16[128,2048]{1,0:T(8,128)(2,1)S(1)}, bf16[128,2048]{1,0:T(8,128)(2,1)}, u32[]{:S(2)}) copy-start(bf16[128,2048]{1,0:T(8,128)(2,1)} %param.10) | copy-start | bytes 1572868
  60.4 212.3 %all-reduce.3.cloned.1.call-start = ((), (), s32[]{:S(2)}) async-start(), calls=%async_computation.4 | async-start | bytes 1048576 | tf_op jit(solution)/shard_map/psum | solution.py:36
  100.9 171.8 %copy-start.2 = (bf16[128,1024]{1,0:T(8,128)(2,1)S(1)}, bf16[128,1024]{1,0:T(8,128)(2,1)}, u32[]{:S(2)}) copy-start(bf16[128,1024]{1,0:T(8,128)(2,1)} %param.17) | copy-start | bytes 786436
  100.9 171.8 %copy-start.3 = (f32[1024]{0:T(1024)S(1)}, f32[1024]{0:T(1024)}, u32[]{:S(2)}) copy-start(f32[1024]{0:T(1024)} %param.16) | copy-start | bytes 12292
  240.6 40.7 %copy-start.1 = (f32[128,2048]{1,0:T(8,128)S(1)}, f32[128,2048]{1,0:T(8,128)}, u32[]{:S(2)}) copy-start(f32[128,2048]{1,0:T(8,128)} %reduce-scatter.2.cloned.1.call-done) | copy-start | bytes 3145732
  244.8 96.1 %all-gather.2.cloned.1.call-start = ((), (), s32[]{:S(2)}) async-start(), calls=%async_computation.5 | async-start | bytes 4456448 | tf_op jit(solution)/shard_map/all_gather | solution.py:41
  275.7 26.8 %all-to-all-start = ((bf16[128,16,128]{0,2,1:T(8,128)(2,1)}), bf16[128,16,128]{0,2,1:T(8,128)(2,1)S(1)}, u32[]{:S(2)}, u32[]{:S(2)}) async-start(bf16[128,16,128]{0,2,1:T(8,128)(2,1)} %bitcast.5), calls=%async_computation.1 | async-start | bytes 1048576 | tf_op jit(solution)/shard_map/all_to_all | solution.py:39
  302.5 44.7 %all-to-all-start.1 = ((bf16[128,16,128]{2,0,1:T(8,128)(2,1)}), bf16[128,16,128]{2,0,1:T(8,128)(2,1)S(1)}, u32[]{:S(2)}, u32[]{:S(2)}) async-start(bf16[128,16,128]{2,0,1:T(8,128)(2,1)} %copy_bitcast_fusion), calls=%async_computation.2 | async-start | bytes 1048576 | tf_op jit(solution)/shard_map/all_to_all | solution.py:40
Sparse Core Ops, SparseCore 0:
  60.5 180.0 reduce-scatter.1
  244.9 27.7 all-reduce.2
  275.4 65.3 all-gather.1

commit v2 on v1

--- a/solution.py
+++ b/solution.py
@@ -26,10 +26,14 @@
         "tkrs,tkb->trbs", tile_bits, source_pick, preferred_element_type=jnp.bfloat16
     )
     mixing = mixing.reshape(targets * block_rows, local_blocks * block_rows)
-    summed_rows = jnp.dot(mixing, features, preferred_element_type=jnp.float32)
-    degree = jnp.sum(mixing, axis=1, dtype=jnp.float32)
-    owner_sums = lax.psum_scatter(summed_rows, "node", scatter_dimension=0, tiled=True)
-    owner_counts = lax.psum_scatter(degree, "node", scatter_dimension=0, tiled=True)
+    feat_cols = features.shape[1]
+    with_ones = jnp.concatenate(
+        [features, jnp.ones((features.shape[0], 128), features.dtype)], axis=1
+    )
+    summed_rows = jnp.dot(mixing, with_ones, preferred_element_type=jnp.float32)
+    owner_all = lax.psum_scatter(summed_rows, "node", scatter_dimension=0, tiled=True)
+    owner_sums = owner_all[:, :feat_cols]
+    owner_counts = owner_all[:, feat_cols]
     aggregate = (owner_sums / jnp.sqrt(1.0 + owner_counts)[:, None]).astype(jnp.bfloat16)
     local_pre = jnp.dot(seed_feats, w_self, preferred_element_type=jnp.float32)
     local_pre = local_pre + jnp.dot(aggregate, w_neigh, preferred_element_type=jnp.float32)

time: 358 us -> 358 us (level)
  waiting for transfers between devices: 220 us -> 265 us
  blocking collectives: 35.6 us -> 0 us
  matrix products: 53.8 us -> 43.8 us
    reduce_scatter x1, waiting for transfers between devices: 140 us -> 185 us  [body(): lax.psum_scatter(summed_rows, 'node', scatter_dimension=0, tiled=True)]
    unnamed x1 -> x0, blocking collectives: 35.6 us -> none
    dot_general x1, matrix products: 17.8 us -> 4.35 us  [body(): jnp.einsum('tkrs,tkb->trbs', tile_bits, source_pick, preferred_element_ty...]
where the time goes in v2:
time: 358 us; the launch traced here: 357 us
  waiting for transfers between devices  265 us (74%)
  matrix products  43.8 us (12%)
  between operations  13.8 us (4%)
  other arithmetic  12.4 us (3%)
  starting transfers between devices  11.4 us (3%)
  local copies, waits for them, and re-layouts  10.2 us (3%)
    reduce_scatter x1, waiting for transfers between devices, body(): lax.psum_scatter(summed_rows, 'node', scatter_dimension=0, tiled=True)  185 us
    all_gather x1, waiting for transfers between devices, body(): grad_all = lax.all_gather(grad_rows, 'node', axis=0, tiled=True)  32.4 us
    psum x1, waiting for transfers between devices, body(): pre_act = lax.psum(local_pre, 'feat')  27.9 us
    dot_general x1, matrix products, body(): summed_rows = jnp.dot(mixing, with_ones, preferred_element_type=jnp.float32)  25.2 us
    all_to_all x1, waiting for transfers between devices, body(): seed_cols = lax.all_to_all(seed_feats, 'node', 1, 0, tiled=True)  20.2 us
  transfers between devices with their start and end apart: 5, of which 4 were waited for; matrix products, arithmetic and copies ran while one was open for 3% of the time, Pallas kernels for 0%

profile of v2, /device:TPU:0, one launch (start us, length us, event | category | flops | bytes accessed | tf_op | source)
XLA Modules:
  0.0 356.9 jit_solution(7848007005078966234)
XLA Ops:
  7.2 0.0 reduce-scatter.2.cloned.1.call-start
  7.2 0.1 shift_right_arithmetic.23
  7.3 0.7 fusion.14
  8.0 5.9 %fusion.6 = bf16[16,8,128,128]{2,3,1,0:T(8,128)(2,1)} fusion(s32[128]{0:T(128)S(1)} %shift_right_arithmetic.23, s32[16,8,128,8]{2,3,1,0:T(8,128)} %param.11, bf16[16,8]{1,0:T(8,128)(2,1)S(1)} %fusion.14), kind=kLoop, calls=%fused_computation.7 | loop fusion | flops 14680064 | bytes 4719360 | tf_op jit(solution)/shard_map/mul | solution.py:21
  13.9 0.0 copy-start.4
  13.9 6.8 %copy.21 = bf16[16,8,128,128]{3,1,2,0:T(8,128)(2,1)} copy(bf16[16,8,128,128]{2,3,1,0:T(8,128)(2,1)} %fusion.6) | data formatting | bytes 8388608 | tf_op jit(solution)/shard_map/mul | solution.py:21
  20.7 0.0 copy-done.4
  20.7 0.1 copy.20
  20.8 4.3 %fusion.11 = bf16[16,16,128,128]{3,1,2,0:T(8,128)(2,1)S(1)} fusion(bf16[16,8,128,128]{3,1,2,0:T(8,128)(2,1)} %copy.21, s32[16,8]{1,0:T(8,128)S(1)} %copy.20), kind=kOutput, calls=%fused_computation.21 | convolution fusion | flops 67110912 | bytes 12583424 | tf_op jit(solution)/shard_map/tkrs,tkb->trbs/dot_general | solution.py:25
  25.1 25.2 %fusion = f32[2048,2176]{1,0:T(8,128)} fusion(bf16[2048,2048]{1,0:T(8,128)(2,1)} %param.9, bf16[256,8,16,128]{3,2,1,0:T(8,128)(2,1)S(1)} %bitcast.41), kind=kOutput, calls=%fused_computation | convolution fusion | flops 18253611008 | bytes 34603008 | tf_op jit(solution)/shard_map/dot_general | solution.py:33
  50.3 0.0 copy-start
  50.3 0.0 reduce-scatter.2.cloned.1.call-update
  50.3 0.0 all-reduce.3.cloned.1.call-start
  50.4 1.0 copy-done
  51.3 2.9 fusion.16
  54.3 184.8 %reduce-scatter.2.cloned.1.call-done = f32[128,2176]{1,0:T(8,128)} async-done(((f32[2048,2176]{1,0:T(8,128)}), f32[128,2176]{1,0:T(8,128)}) %reduce-scatter.2.cloned.1.call-update) | async-done | bytes 1114128 | tf_op jit(solution)/shard_map/reduce_scatter | solution.py:34
  239.0 0.9 fusion.9
  240.0 0.0 copy-start.2
  240.0 0.0 copy-start.3
  240.0 0.0 copy-start.1
  240.0 4.2 %convolution_add_fusion = f32[128,1024]{1,0:T(8,128)} fusion(f32[128,1024]{1,0:T(8,128)S(1)} %fusion.16, bf16[2048,1024]{1,0:T(8,128)(2,1)} %param.15, f32[128,2176]{1,0:T(8,128)} %reduce-scatter.2.cloned.1.call-done, f32[128]{0:T(128)S(1)} %fusion.9), kind=kOutput, calls=%fused_computation.8 | convolution fusion | flops 537526272 | bytes 6291968 | tf_op jit(solution)/shard_map/dot_general | solution.py:39
  244.2 0.0 all-reduce.3.cloned.1.call-update
  244.2 0.0 all-gather.2.cloned.1.call-start
  244.2 27.9 %all-reduce.3.cloned.1.call-done = f32[128,1024]{1,0:T(8,128)} async-done(((f32[128,1024]{1,0:T(8,128)}), f32[128,1024]{1,0:T(8,128)}) %all-reduce.3.cloned.1.call-update) | async-done | bytes 524304 | tf_op jit(solution)/shard_map/psum | solution.py:40
  272.1 0.0 copy-done.2
  272.1 0.0 copy-done.3
  272.1 2.0 compare_select_fusion
  274.1 0.0 all-gather.2.cloned.1.call-update
  274.1 1.0 copy.22
  275.1 5.6 %all-to-all-start = ((bf16[128,16,128]{0,2,1:T(8,128)(2,1)}), bf16[128,16,128]{0,2,1:T(8,128)(2,1)S(1)}, u32[]{:S(2)}, u32[]{:S(2)}) async-start(bf16[128,16,128]{0,2,1:T(8,128)(2,1)} %bitcast.4), calls=%async_computation.1 | async-start | bytes 1048576 | tf_op jit(solution)/shard_map/all_to_all | solution.py:43
  280.7 0.0 copy-done.1
  280.7 1.0 copy_bitcast_fusion
  281.7 20.2 %all-to-all-done = bf16[128,16,128]{0,2,1:T(8,128)(2,1)S(1)} async-done(((bf16[128,16,128]{0,2,1:T(8,128)(2,1)}), bf16[128,16,128]{0,2,1:T(8,128)(2,1)S(1)}, u32[]{:S(2)}, u32[]{:S(2)}) %all-to-all-start) | async-done | bytes 524320 | tf_op jit(solution)/shard_map/all_to_all | solution.py:43
  301.9 5.6 %all-to-all-start.1 = ((bf16[128,16,128]{2,0,1:T(8,128)(2,1)}), bf16[128,16,128]{2,0,1:T(8,128)(2,1)S(1)}, u32[]{:S(2)}, u32[]{:S(2)}) async-start(bf16[128,16,128]{2,0,1:T(8,128)(2,1)} %copy_bitcast_fusion), calls=%async_computation.2 | async-start | bytes 1048576 | tf_op jit(solution)/shard_map/all_to_all | solution.py:44
  307.6 0.3 copy.23
  307.9 32.4 %all-gather.2.cloned.1.call-done = bf16[2048,1024]{1,0:T(8,128)(2,1)} async-done(((bf16[128,1024]{1,0:T(8,128)(2,1)}), bf16[2048,1024]{1,0:T(8,128)(2,1)}) %all-gather.2.cloned.1.call-update) | async-done | bytes 4194320 | tf_op jit(solution)/shard_map/all_gather | solution.py:45
  340.3 3.5 convolution_bitcast_fusion
  343.8 1.0 copy.25
  344.8 1.9 convert_reduce_fusion
  346.7 0.0 all-to-all-done.1
  346.7 3.7 %fusion.17 = f32[128,1024]{1,0:T(8,128)} fusion(bf16[2048,128]{1,0:T(8,128)(2,1)S(1)} %bitcast.42, bf16[2048,1024]{1,0:T(8,128)(2,1)} %all-gather.2.cloned.1.call-done), kind=kOutput, calls=%fused_computation.27 | convolution fusion | flops 536870912 | bytes 5242880 | tf_op jit(solution)/shard_map/dot_general | solution.py:50
  (1 shorter events, 0.0 us)
Async XLA Ops:
  7.2 231.8 %reduce-scatter.2.cloned.1.call-start = ((), (), s32[]{:S(2)}) async-start(), calls=%async_computation.3 | async-start | bytes 18939904 | tf_op jit(solution)/shard_map/reduce_scatter | solution.py:34
  13.9 6.8 %copy-start.4 = (s32[16,8]{0,1:T(8,128)S(1)}, s32[16,8]{0,1:T(8,128)}, u32[]{:S(2)}) copy-start(s32[16,8]{0,1:T(8,128)} %param.12) | copy-start | bytes 1540
  50.3 1.0 copy-start
  50.3 221.8 %all-reduce.3.cloned.1.call-start = ((), (), s32[]{:S(2)}) async-start(), calls=%async_computation.4 | async-start | bytes 1048576 | tf_op jit(solution)/shard_map/psum | solution.py:40
  240.0 32.2 %copy-start.2 = (bf16[128,1024]{1,0:T(8,128)(2,1)S(1)}, bf16[128,1024]{1,0:T(8,128)(2,1)}, u32[]{:S(2)}) copy-start(bf16[128,1024]{1,0:T(8,128)(2,1)} %param.17) | copy-start | bytes 786436
  240.0 32.2 %copy-start.3 = (f32[1024]{0:T(1024)S(1)}, f32[1024]{0:T(1024)}, u32[]{:S(2)}) copy-start(f32[1024]{0:T(1024)} %param.16) | copy-start | bytes 12292
  240.0 40.7 %copy-start.1 = (f32[128,2176]{1,0:T(8,128)S(1)}, f32[128,2176]{1,0:T(8,128)}, u32[]{:S(2)}) copy-start(f32[128,2176]{1,0:T(8,128)} %reduce-scatter.2.cloned.1.call-done) | copy-start | bytes 3342340
  244.2 96.1 %all-gather.2.cloned.1.call-start = ((), (), s32[]{:S(2)}) async-start(), calls=%async_computation.5 | async-start | bytes 4456448 | tf_op jit(solution)/shard_map/all_gather | solution.py:45
  275.1 26.8 %all-to-all-start = ((bf16[128,16,128]{0,2,1:T(8,128)(2,1)}), bf16[128,16,128]{0,2,1:T(8,128)(2,1)S(1)}, u32[]{:S(2)}, u32[]{:S(2)}) async-start(bf16[128,16,128]{0,2,1:T(8,128)(2,1)} %bitcast.4), calls=%async_computation.1 | async-start | bytes 1048576 | tf_op jit(solution)/shard_map/all_to_all | solution.py:43
  301.9 44.7 %all-to-all-start.1 = ((bf16[128,16,128]{2,0,1:T(8,128)(2,1)}), bf16[128,16,128]{2,0,1:T(8,128)(2,1)S(1)}, u32[]{:S(2)}, u32[]{:S(2)}) async-start(bf16[128,16,128]{2,0,1:T(8,128)(2,1)} %copy_bitcast_fusion), calls=%async_computation.2 | async-start | bytes 1048576 | tf_op jit(solution)/shard_map/all_to_all | solution.py:44
Sparse Core Ops, SparseCore 0:
  50.5 188.5 reduce-scatter.1
  244.3 27.7 all-reduce.2
  274.9 65.3 all-gather.1

commit v3 on v1

--- a/solution.py
+++ b/solution.py
@@ -28,7 +28,9 @@
     mixing = mixing.reshape(targets * block_rows, local_blocks * block_rows)
     summed_rows = jnp.dot(mixing, features, preferred_element_type=jnp.float32)
     degree = jnp.sum(mixing, axis=1, dtype=jnp.float32)
-    owner_sums = lax.psum_scatter(summed_rows, "node", scatter_dimension=0, tiled=True)
+    parts = lax.all_to_all(summed_rows, "node", 0, 0, tiled=True)
+    owner_rows = parts.shape[0] // n_node
+    owner_sums = jnp.sum(parts.reshape(n_node, owner_rows, parts.shape[1]), axis=0)
     owner_counts = lax.psum_scatter(degree, "node", scatter_dimension=0, tiled=True)
     aggregate = (owner_sums / jnp.sqrt(1.0 + owner_counts)[:, None]).astype(jnp.bfloat16)
     local_pre = jnp.dot(seed_feats, w_self, preferred_element_type=jnp.float32)

time: 358 us -> 594 us (1.66)
  blocking collectives: 35.6 us -> 329 us
  waiting for transfers between devices: 220 us -> 131 us
  local copies, waits for them, and re-layouts: 10.4 us -> 23.7 us
  other arithmetic: 11.6 us -> 18.9 us
  starting transfers between devices: 11.4 us -> 18.6 us
    unnamed x1, blocking collectives: 35.6 us -> 329 us
    reduce_scatter x1 -> x0, waiting for transfers between devices: 140 us -> none  [body(): lax.psum_scatter(summed_rows, 'node', scatter_dimension=0, tiled=True)]
    psum x1, waiting for transfers between devices: 27.9 us -> 78.7 us  [body(): pre_act = lax.psum(local_pre, 'feat')]
    all_gather x1, waiting for transfers between devices: 32.4 us -> 9.45 us  [body(): grad_all = lax.all_gather(grad_rows, 'node', axis=0, tiled=True)]
    all_to_all x1, waiting for transfers between devices: 0.01 us -> 22.7 us  [body(): agg_cols = lax.all_to_all(aggregate, 'node', 1, 0, tiled=True)]
    dot_general x0 -> x1, local copies, waits for them, and re-layouts: none -> 13.3 us  [body(): summed_rows = jnp.dot(mixing, features, preferred_element_type=jnp.float32)]
    all_to_all x0 -> x1, starting transfers between devices: none -> 7.57 us  [body(): parts = lax.all_to_all(summed_rows, 'node', 0, 0, tiled=True)]
    reduce_sum x0 -> x1, other arithmetic: none -> 7.45 us  [body(): jnp.sum(parts.reshape(n_node, owner_rows, parts.shape[1]), axis=0)]
  transfers between devices with their start and end apart: 5 -> 5, of which waited for: 4 -> 4; matrix products, arithmetic and copies ran while one was open for 3% -> 1% of each run, Pallas kernels for 0% -> 0%
where the time goes in v3:
time: 594 us; the launch traced here: 593 us
  blocking collectives  329 us (55%)
  waiting for transfers between devices  131 us (22%)
  matrix products  56.9 us (10%)
  local copies, waits for them, and re-layouts  23.7 us (4%)
  other arithmetic  18.9 us (3%)
  starting transfers between devices  18.6 us (3%)
  between operations  14.8 us (2%)
    unnamed x1, blocking collectives  329 us
    psum x1, waiting for transfers between devices, body(): pre_act = lax.psum(local_pre, 'feat')  78.7 us
    dot_general x1, matrix products, body(): summed_rows = jnp.dot(mixing, features, preferred_element_type=jnp.float32)  24.2 us
    all_to_all x1, waiting for transfers between devices, body(): agg_cols = lax.all_to_all(aggregate, 'node', 1, 0, tiled=True)  22.7 us
    all_to_all x1, waiting for transfers between devices, body(): seed_cols = lax.all_to_all(seed_feats, 'node', 1, 0, tiled=True)  20.3 us
    dot_general x1, matrix products, body(): jnp.einsum('tkrs,tkb->trbs', tile_bits, source_pick, preferred_element_ty...  18.8 us
    dot_general x1, local copies, waits for them, and re-layouts, body(): summed_rows = jnp.dot(mixing, features, preferred_element_type=jnp.float32)  13.3 us
  transfers between devices with their start and end apart: 5, of which 4 were waited for; matrix products, arithmetic and copies ran while one was open for 1% of the time, Pallas kernels for 0%

profile of v3, /device:TPU:0, one launch (start us, length us, event | category | flops | bytes accessed | tf_op | source)
XLA Modules:
  0.0 593.3 jit_solution(4619825863847857370)
XLA Ops:
  7.2 0.1 shift_right_arithmetic.23
  7.3 0.7 fusion.9
  8.0 5.9 fusion.4
  13.9 0.0 copy-start.3
  13.9 6.7 %copy.26 = bf16[16,8,128,128]{3,1,2,0:T(8,128)(2,1)} copy(bf16[16,8,128,128]{2,3,1,0:T(8,128)(2,1)} %fusion.4) | data formatting | bytes 8388608 | tf_op jit(solution)/shard_map/mul | solution.py:21
  20.6 0.0 copy-done.3
  20.6 0.1 copy.25
  20.7 18.8 %convert_reduce_fusion = (f32[16,128]{1,0:T(8,128)S(1)}, bf16[16,128,16,128]{3,2,1,0:T(8,128)(2,1)}) fusion(bf16[16,8,128,128]{3,1,2,0:T(8,128)(2,1)} %copy.26, s32[16,8]{1,0:T(8,128)S(1)} %copy.25), kind=kOutput, calls=%fused_computation | convolution fusion | flops 75497472 | bytes 12591616 | tf_op jit(solution)/shard_map/tkrs,tkb->trbs/dot_general | solution.py:25
  39.4 13.3 %dot_general.24 = bf16[16,128,2048]{2,1,0:T(8,128)(2,1)} reshape(bf16[16,128,16,128]{3,2,1,0:T(8,128)(2,1)} %get-tuple-element.23) | data formatting | bytes 16777216 | tf_op jit(solution)/shard_map/dot_general | solution.py:29
  52.8 24.2 %fusion = f32[16,128,2048]{2,1,0:T(8,128)} fusion(bf16[16,128,2048]{2,1,0:T(8,128)(2,1)} %dot_general.24, bf16[2048,2048]{1,0:T(8,128)(2,1)} %param.9), kind=kOutput, calls=%fused_computation.1 | convolution fusion | flops 17179869184 | bytes 33554432 | tf_op jit(solution)/shard_map/dot_general | solution.py:29
  77.0 0.0 copy-start.4
  77.0 0.0 copy-start
  77.0 7.6 %all-to-all-start = ((f32[16,128,2048]{2,1,0:T(8,128)}), f32[16,128,2048]{2,1,0:T(8,128)}, u32[]{:S(2)}, u32[]{:S(2)}) async-start(f32[16,128,2048]{2,1,0:T(8,128)} %fusion), calls=%async_computation | async-start | bytes 33554432 | tf_op jit(solution)/shard_map/all_to_all | solution.py:31
  84.6 0.0 all-reduce.3.cloned.1.call-start
  84.6 0.0 copy-done.4
  84.6 0.6 dynamic-slice
  85.9 329.3 %all-reduce = f32[2048]{0:T(1024)S(1)} all-reduce(f32[2048]{0:T(1024)S(1)} %bitcast.46), channel_id=2, replica_groups=mesh['feat'=2,'node'=16] {'node'}, use_global_device_ids=true, to_apply=%region_2.0.clone | all-reduce | flops 2048 | bytes 16384
  415.2 0.1 fusion.10
  415.2 0.0 copy-done
  415.3 2.9 fusion.11
  418.2 0.0 all-to-all-done
  418.2 7.4 %reduce_sum.31 = f32[128,2048]{1,0:T(8,128)S(1)} reduce(f32[16,128,2048]{2,1,0:T(8,128)} %all-to-all-done, f32[]{:T(128)} %constant.9.clone.1), dimensions={0}, to_apply=%region_0.0 | reduce | flops 3932160 | bytes 17825796 | tf_op jit(solution)/shard_map/reduce_sum | solution.py:33
  425.6 0.0 copy-start.1
  425.6 0.0 copy-start.2
  425.6 3.8 convolution_add_fusion
  429.4 0.0 all-reduce.3.cloned.1.call-update
  429.5 0.0 all-gather.2.cloned.1.call-start
  429.5 78.7 %all-reduce.3.cloned.1.call-done = f32[128,1024]{1,0:T(8,128)} async-done(((f32[128,1024]{1,0:T(8,128)}), f32[128,1024]{1,0:T(8,128)}) %all-reduce.3.cloned.1.call-update) | async-done | bytes 524304 | tf_op jit(solution)/shard_map/psum | solution.py:38
  508.2 0.0 copy-done.1
  508.2 0.0 copy-done.2
  508.2 2.0 compare_select_fusion
  510.2 0.0 all-gather.2.cloned.1.call-update
  510.2 1.0 copy.27
  511.2 5.6 all-to-all-start.1
  516.8 0.3 copy.29
  517.1 0.9 divide_convert_fusion
  518.1 20.3 %all-to-all-done.1 = bf16[128,16,128]{0,2,1:T(8,128)(2,1)S(1)} async-done(((bf16[128,16,128]{0,2,1:T(8,128)(2,1)}), bf16[128,16,128]{0,2,1:T(8,128)(2,1)S(1)}, u32[]{:S(2)}, u32[]{:S(2)}) %all-to-all-start.1) | async-done | bytes 524320 | tf_op jit(solution)/shard_map/all_to_all | solution.py:41
  538.3 5.3 all-to-all-start.2
  543.6 0.3 copy.28
  543.9 22.7 %all-to-all-done.2 = bf16[128,16,128]{0,2,1:T(8,128)(2,1)S(1)} async-done(((bf16[128,16,128]{0,2,1:T(8,128)(2,1)}), bf16[128,16,128]{0,2,1:T(8,128)(2,1)S(1)}, u32[]{:S(2)}, u32[]{:S(2)}) %all-to-all-start.2) | async-done | bytes 524320 | tf_op jit(solution)/shard_map/all_to_all | solution.py:42
  566.6 0.3 copy.30
  566.9 9.5 %all-gather.2.cloned.1.call-done = bf16[2048,1024]{1,0:T(8,128)(2,1)} async-done(((bf16[128,1024]{1,0:T(8,128)(2,1)}), bf16[2048,1024]{1,0:T(8,128)(2,1)}) %all-gather.2.cloned.1.call-update) | async-done | bytes 4194320 | tf_op jit(solution)/shard_map/all_gather | solution.py:43
  576.4 3.5 convolution_bitcast_fusion.1
  579.8 1.0 copy.31
  580.8 1.9 convert_reduce_fusion.1
  582.7 3.7 fusion.12
  (1 shorter events, 0.0 us)
Async XLA Ops:
  13.9 6.7 %copy-start.3 = (s32[16,8]{0,1:T(8,128)S(1)}, s32[16,8]{0,1:T(8,128)}, u32[]{:S(2)}) copy-start(s32[16,8]{0,1:T(8,128)} %param.12) | copy-start | bytes 1540
  77.0 7.6 %copy-start.4 = (u32[32]{0:T(128)S(1)}, u32[32]{0:T(128)}, u32[]{:S(2)}) copy-start(u32[32]{0:T(128)} %constant.21) | copy-start | bytes 388
  77.0 338.3 %copy-start = (bf16[128,2048]{1,0:T(8,128)(2,1)S(1)}, bf16[128,2048]{1,0:T(8,128)(2,1)}, u32[]{:S(2)}) copy-start(bf16[128,2048]{1,0:T(8,128)(2,1)} %param.10) | copy-start | bytes 1572868
  77.0 341.2 %all-to-all-start = ((f32[16,128,2048]{2,1,0:T(8,128)}), f32[16,128,2048]{2,1,0:T(8,128)}, u32[]{:S(2)}, u32[]{:S(2)}) async-start(f32[16,128,2048]{2,1,0:T(8,128)} %fusion), calls=%async_computation | async-start | bytes 33554432 | tf_op jit(solution)/shard_map/all_to_all | solution.py:31
  84.6 423.6 %all-reduce.3.cloned.1.call-start = ((), (), s32[]{:S(2)}) async-start(), calls=%async_computation.3 | async-start | bytes 1048576 | tf_op jit(solution)/shard_map/psum | solution.py:38
  425.6 82.6 %copy-start.1 = (bf16[128,1024]{1,0:T(8,128)(2,1)S(1)}, bf16[128,1024]{1,0:T(8,128)(2,1)}, u32[]{:S(2)}) copy-start(bf16[128,1024]{1,0:T(8,128)(2,1)} %param.17) | copy-start | bytes 786436
  425.6 82.6 %copy-start.2 = (f32[1024]{0:T(1024)S(1)}, f32[1024]{0:T(1024)}, u32[]{:S(2)}) copy-start(f32[1024]{0:T(1024)} %param.16) | copy-start | bytes 12292
  429.5 146.9 %all-gather.2.cloned.1.call-start = ((), (), s32[]{:S(2)}) async-start(), calls=%async_computation.4 | async-start | bytes 4456448 | tf_op jit(solution)/shard_map/all_gather | solution.py:43
  511.2 27.1 %all-to-all-start.1 = ((bf16[128,16,128]{0,2,1:T(8,128)(2,1)}), bf16[128,16,128]{0,2,1:T(8,128)(2,1)S(1)}, u32[]{:S(2)}, u32[]{:S(2)}) async-start(bf16[128,16,128]{0,2,1:T(8,128)(2,1)} %bitcast.6), calls=%async_computation.1 | async-start | bytes 1048576 | tf_op jit(solution)/shard_map/all_to_all | solution.py:41
  538.3 28.3 %all-to-all-start.2 = ((bf16[128,16,128]{0,2,1:T(8,128)(2,1)}), bf16[128,16,128]{0,2,1:T(8,128)(2,1)S(1)}, u32[]{:S(2)}, u32[]{:S(2)}) async-start(bf16[128,16,128]{0,2,1:T(8,128)(2,1)} %divide_convert_fusion), calls=%async_computation.2 | async-start | bytes 1048576 | tf_op jit(solution)/shard_map/all_to_all | solution.py:42
Sparse Core Ops, SparseCore 0:
  429.6 78.5 all-reduce.2
  510.4 65.9 all-gather.1
